TPU v7x, 256 devices: a whole 4x4x8 slice. The times are simulated.
256 devices in a mesh: snap: 8 (over z), py: 4 (over y_lo, core), pz: 8 (over y_hi, x).
Axes of the slice: x: 4, y: 4 (y_hi: 2, y_lo: 2; y = y_hi * 2 + y_lo), z: 8, core: 2. Of those that a mesh axis runs over, the one named last changes fastest.
Arguments:
- velocity: bfloat16 [8, 3, 48, 384, 1024], P('snap', None, 'pz', 'py'), may hold values from -6 to 6
- metric_x: float32 [1024], replicated, may hold values from 0.5 to 2
- metric_y: float32 [384], replicated, may hold values from 0.3 to 3
- metric_z: float32 [48], replicated, may hold values from 0.5 to 2
- sketch_matrix: float32 [8, 4], replicated, may hold values from -2 to 2
Outputs:
- sketch: float32 [4, 3, 48, 384, 1024], P(None, None, None, ('snap', 'pz'), 'py')
All inputs are finite; a program needn't handle non-finite values.
Results may differ from a plain program's by a relative error of at most 0.0065.
Values may be sent and summed in bfloat16 or wider, within the bound.
A program may use at most 128 MiB of HBM per device.

v0:
```python
import jax
import jax.numpy as jnp
from jax import lax
from jax.sharding import PartitionSpec as P

log_ratio = jnp.log((3.0 - 5.0**0.5) / 2.0)
scale_const = 5.0**0.5 / 3.0


def inverse_entry(row_index, col_index, length):
    inside = (col_index >= 0) & (col_index < length)
    column = jnp.clip(col_index, 0, length - 1)
    nearer = jnp.minimum(row_index, column).astype(jnp.float32)
    farther = jnp.maximum(row_index, column).astype(jnp.float32)
    distance = farther - nearer
    parity_sign = 1.0 - 2.0 * jnp.mod(distance, 2.0)
    magnitude = jnp.exp(distance * log_ratio) * parity_sign
    left_factor = 1.0 - jnp.exp(2.0 * (nearer + 1.0) * log_ratio)
    right_factor = 1.0 - jnp.exp(2.0 * (length - farther) * log_ratio)
    denominator = scale_const * (1.0 - jnp.exp(2.0 * (length + 1.0) * log_ratio))
    return jnp.where(inside, magnitude * left_factor * right_factor / denominator, 0.0)


def compact_table(length):
    row_index = lax.broadcasted_iota(jnp.int32, (length, length), 0)
    col_index = lax.broadcasted_iota(jnp.int32, (length, length), 1)
    first = inverse_entry(row_index, col_index - 1, length) - inverse_entry(
        row_index, col_index + 1, length
    )
    second = inverse_entry(row_index, col_index - 2, length) - inverse_entry(
        row_index, col_index + 2, length
    )
    return 7.0 / 9.0 * first + 1.0 / 36.0 * second


def split_table(length):
    table = compact_table(length)
    table_high = table.astype(jnp.bfloat16)
    table_low = (table - table_high.astype(jnp.float32)).astype(jnp.bfloat16)
    return (table_high, table_low)


def apply_split(form, tables, fields, table_first):
    table_high, table_low = tables
    if table_first:
        high_part = jnp.einsum(form, table_high, fields, preferred_element_type=jnp.float32)
        low_part = jnp.einsum(form, table_low, fields, preferred_element_type=jnp.float32)
    else:
        high_part = jnp.einsum(form, fields, table_high, preferred_element_type=jnp.float32)
        low_part = jnp.einsum(form, fields, table_low, preferred_element_type=jnp.float32)
    return high_part + low_part


def vorticity_from(zlines, metric_z):
    tables_z = split_table(zlines.shape[2])
    z_slopes = apply_split("ij,scjyx->sciyx", tables_z, zlines[:, 0:2], True)
    z_slopes = z_slopes * metric_z[None, None, :, None, None]
    slope_uz = z_slopes[:, 0]
    slope_vz = z_slopes[:, 1]
    slope_wx = zlines[:, 2].astype(jnp.float32)
    slope_wy = zlines[:, 3].astype(jnp.float32)
    spin_x = (slope_wy - slope_vz).astype(jnp.bfloat16)
    spin_y = (slope_uz - slope_wx).astype(jnp.bfloat16)
    return jnp.stack([spin_x, spin_y, zlines[:, 4]], axis=1)


def on_device(velocity, metric_x, metric_y, metric_z, sketch_matrix):
    tables_x = split_table(velocity.shape[4])
    x_slopes = apply_split("sczyj,ij->sczyi", tables_x, velocity[:, 1:3], False)
    x_slopes = (x_slopes * metric_x).astype(jnp.bfloat16)
    payload = jnp.concatenate([velocity, x_slopes], axis=1)
    ylines = lax.all_to_all(payload, "py", split_axis=4, concat_axis=3, tiled=True)
    tables_y = split_table(ylines.shape[3])
    y_slopes = apply_split("ij,sczjx->sczix", tables_y, ylines[:, 0:3:2], True)
    y_slopes = y_slopes * metric_y[None, None, None, :, None]
    slope_uy = y_slopes[:, 0]
    slope_wy = y_slopes[:, 1].astype(jnp.bfloat16)
    spin_z = (ylines[:, 3].astype(jnp.float32) - slope_uy).astype(jnp.bfloat16)
    z_payload = jnp.stack([ylines[:, 0], ylines[:, 1], ylines[:, 4], slope_wy, spin_z], axis=1)
    zlines = lax.all_to_all(
        lax.all_to_all(z_payload, "snap", split_axis=3, concat_axis=0, tiled=True),
        "pz",
        split_axis=3,
        concat_axis=2,
        tiled=True,
    )
    vorticity = vorticity_from(zlines, metric_z)
    return jnp.einsum(
        "sk,sczyx->kczyx",
        sketch_matrix,
        vorticity.astype(jnp.float32),
        precision=lax.Precision.HIGHEST,
    )


def solution(mesh):
    placed = (P("snap", None, "pz", "py", None), P(), P(), P(), P())
    return jax.shard_map(
        on_device,
        mesh=mesh,
        in_specs=placed,
        out_specs=P(None, None, None, ("snap", "pz"), "py"),
        check_vma=False,
    )
```

profile of v0, /device:TPU:30, one launch (start us, length us, event | category | flops | bytes accessed | tf_op | source)
XLA Modules:
  0.0 559.7 jit_solution(15133581711998774805)
XLA Ops:
  0.0 0.0 copy-start
  0.0 0.6 fusion.361
  0.6 0.6 fusion.367
  1.2 0.6 fusion.369
  1.8 8.1 %copy.36 = bf16[1,3,6,96,1024]{3,2,1,0,4:T(8,128)(2,1)} copy(bf16[1,3,6,96,1024]{4,3,2,1,0:T(8,128)(2,1)} %param.6) | data formatting | bytes 7077888 | tf_op args[0]
  10.0 0.0 copy-start.10
  10.0 29.3 %fusion.112 = f32[1024,2,6,96]{0,3,2,1:T(8,128)S(1)} fusion(s32[1024]{0:T(1024)S(1)} %get-tuple-element.12, s32[1024]{0:T(1024)S(1)} %get-tuple-element.13, s32[1024]{0:T(1024)S(1)} %get-tuple-element.14, s32[1024]{0:T(1024)} %get-tuple-element.15, pred[1024]{0:T(1024)(128)(4,1)} %get-tuple-element.19, pred[1024]{0:T(1024)(128)(4,1)} %get-tuple-element.18, ...), kind=kOutput, calls=%fused_computation.135 | convolution fusion | flops 2530213888 | bytes 7098368 | tf_op jit(solution)/shard_map/sczyj,ij->sczyi/dot_general | solution.py:50
  39.3 28.4 %fusion.104 = bf16[1,2,6,96,1024]{4,3,2,1,0:T(8,128)(2,1)} fusion(f32[1024,2,6,96]{0,3,2,1:T(8,128)S(1)} %fusion.112, f32[1024]{0:T(1024)S(1)} %copy-done.10, bf16[1,3,6,96,1024]{4,3,2,1,0:T(8,128)(2,1)S(1)} %copy-done.2, s32[1024]{0:T(1024)S(1)} %get-tuple-element.12, pred[1024]{0:T(1024)(128)(4,1)S(1)} %copy-done.8, s32[1024]{0:T(1024)S(1)} %get-tuple-element.13, ...), kind=kOutput, calls=%fused_computation.123 | convolution fusion | flops 2530607104 | bytes 9461760 | tf_op jit(solution)/shard_map/sczyj,ij->sczyi/dot_general | solution.py:49
  67.7 6.5 %copy.37 = bf16[1,2,6,96,1024]{3,2,1,0,4:T(8,128)(2,1)} copy(bf16[1,2,6,96,1024]{4,3,2,1,0:T(8,128)(2,1)} %fusion.104) | data formatting | bytes 4718592 | tf_op jit(solution)/shard_map/convert_element_type | solution.py:70
  74.2 10.8 %pad_maximum_fusion = bf16[1,5,6,96,1024]{3,2,1,0,4:T(8,128)(2,1)} fusion(bf16[1,2,6,96,1024]{3,2,1,0,4:T(8,128)(2,1)} %copy.37, bf16[1,3,6,96,1024]{3,2,1,0,4:T(8,128)(2,1)} %copy.36), kind=kLoop, calls=%fused_computation | loop fusion | flops 2949120 | bytes 11796480 | tf_op jit(solution)/shard_map/concatenate | solution.py:71
  85.0 6.8 %all-to-all-start = ((bf16[1,5,6,96,1024]{3,2,1,0,4:T(8,128)(2,1)}), bf16[1,5,6,96,1024]{3,2,1,0,4:T(8,128)(2,1)}, u32[]{:S(2)}, u32[]{:S(2)}) async-start(bf16[1,5,6,96,1024]{3,2,1,0,4:T(8,128)(2,1)} %pad_maximum_fusion), calls=%async_computation | async-start | bytes 20971520 | tf_op jit(solution)/shard_map/all_to_all | solution.py:72
  91.8 0.6 fusion.384
  92.4 0.6 fusion.386
  92.9 0.6 fusion.378
  93.5 112.3 %all-to-all-done = bf16[1,5,6,96,1024]{3,2,1,0,4:T(8,128)(2,1)} async-done(((bf16[1,5,6,96,1024]{3,2,1,0,4:T(8,128)(2,1)}), bf16[1,5,6,96,1024]{3,2,1,0,4:T(8,128)(2,1)}, u32[]{:S(2)}, u32[]{:S(2)}) %all-to-all-start) | async-done | bytes 5898272 | tf_op jit(solution)/shard_map/all_to_all | solution.py:72
  205.8 12.4 %copy.62 = bf16[1,5,6,96,4,256]{5,4,3,2,1,0:T(4,128)(2,1)} copy(bf16[1,5,6,96,4,256]{3,2,1,5,4,0:T(8,128)(2,1)} %bitcast.7) | data formatting | bytes 11796480 | tf_op jit(solution)/shard_map/all_to_all | solution.py:72
  218.2 3.9 copy.39
  222.0 1.7 fusion.447
  223.7 0.2 slice.55
  223.9 1.4 copy-done.1
  225.3 1.7 copy.66
  227.0 0.0 copy-start.11
  227.1 6.2 %fusion.108 = f32[2,6,256,384]{3,2,1,0:T(8,128)S(1)} fusion(bf16[1,5,6,384,256]{4,3,2,1,0:T(8,128)(2,1)} %bitcast.84, s32[384]{0:T(512)S(1)} %get-tuple-element.20, s32[384]{0:T(512)S(1)} %get-tuple-element.21, s32[384]{0:T(512)S(1)} %get-tuple-element.22, s32[384]{0:T(512)} %get-tuple-element.23, pred[384]{0:T(512)(128)(4,1)} %get-tuple-element.27, ...), kind=kOutput, calls=%fused_computation.131 | convolution fusion | flops 922042368 | bytes 7086592 | tf_op jit(solution)/shard_map/ij,sczjx->sczix/dot_general | solution.py:47
  233.3 0.0 copy-done.4
  233.3 0.0 copy-done.11
  233.3 0.0 copy-done.12
  233.4 6.4 %fusion = f32[1,2,6,384,256]{3,4,2,1,0:T(8,128)S(1)} fusion(f32[2,6,256,384]{3,2,1,0:T(8,128)S(1)} %fusion.108, f32[384]{0:T(512)S(1)} %copy-done.11, bf16[1,5,6,384,256]{4,3,2,1,0:T(8,128)(2,1)} %bitcast.85, s32[384]{0:T(512)S(1)} %get-tuple-element.20, pred[384]{0:T(512)(128)(4,1)S(1)} %copy-done.15, s32[384]{0:T(512)S(1)} %get-tuple-element.21, ...), kind=kOutput, calls=%fused_computation.15 | convolution fusion | flops 923959296 | bytes 11805696 | tf_op jit(solution)/shard_map/ij,sczjx->sczix/dot_general | solution.py:46
  239.8 1.2 slice.94
  240.9 1.4 fusion.107
  242.3 1.6 copy.43
  243.9 2.4 copy.42
  246.2 4.8 pad_maximum_fusion.1
  251.0 6.2 %copy.44 = bf16[1,5,6,384,256]{4,2,1,0,3:T(8,128)(2,1)S(1)} copy(bf16[1,5,6,384,256]{4,3,2,1,0:T(8,128)(2,1)} %pad_maximum_fusion.1) | data formatting | bytes 11796480 | tf_op jit(solution)/shard_map/stack | solution.py:79
  257.2 183.2 %all_to_all.54 = bf16[1,5,6,384,256]{4,2,1,0,3:T(8,128)(2,1)} all-to-all(bf16[1,5,6,384,256]{4,2,1,0,3:T(8,128)(2,1)S(1)} %copy.44), channel_id=1, replica_groups=mesh['snap'=8,'py'=4,'pz'=8] {'snap'}, dimensions={3} | all-to-all | bytes 11796480 | tf_op jit(solution)/shard_map/all_to_all | solution.py:81
  440.4 12.2 %copy.46 = bf16[8,5,6,48,256]{4,0,2,1,3:T(8,128)(2,1)} copy(bf16[8,5,6,48,256]{4,2,1,3,0:T(8,128)(2,1)} %bitcast.78) | data formatting | bytes 11796480 | tf_op jit(solution)/shard_map/all_to_all | solution.py:81
  452.7 7.5 %all-to-all-start.2 = ((bf16[8,5,6,48,256]{4,0,2,1,3:T(8,128)(2,1)}), bf16[8,5,6,48,256]{4,0,2,1,3:T(8,128)(2,1)}, u32[]{:S(2)}, u32[]{:S(2)}) async-start(bf16[8,5,6,48,256]{4,0,2,1,3:T(8,128)(2,1)} %copy.46), calls=%async_computation.2 | async-start | bytes 11796480 | tf_op jit(solution)/shard_map/all_to_all | solution.py:80
  460.2 81.9 %all-to-all-done.2 = bf16[8,5,6,48,256]{4,0,2,1,3:T(8,128)(2,1)} async-done(((bf16[8,5,6,48,256]{4,0,2,1,3:T(8,128)(2,1)}), bf16[8,5,6,48,256]{4,0,2,1,3:T(8,128)(2,1)}, u32[]{:S(2)}, u32[]{:S(2)}) %all-to-all-start.2) | async-done | bytes 5898272 | tf_op jit(solution)/shard_map/all_to_all | solution.py:80
  542.1 3.3 copy.48
  545.4 0.2 slice.61
  545.6 0.2 fusion.446
  545.8 0.4 copy.70
  546.3 0.0 copy-start.9
  546.3 2.1 fusion.123
  548.4 2.2 multiply_bitcast_fusion
  550.6 1.3 fusion.106
  551.9 0.4 pad_maximum_fusion.2
  552.4 4.0 fusion.130
  556.4 2.9 copy.54
  (30 shorter events, 0.1 us)
Async XLA Ops:
  0.0 552.4 %copy-start = (f32[8,4]{0,1:T(4,128)S(1)}, f32[8,4]{0,1:T(4,128)}, u32[]{:S(2)}) copy-start(f32[8,4]{0,1:T(4,128)} %param.10) | copy-start | bytes 388
  1.8 8.1 %copy-start.2 = (bf16[1,3,6,96,1024]{4,3,2,1,0:T(8,128)(2,1)S(1)}, bf16[1,3,6,96,1024]{4,3,2,1,0:T(8,128)(2,1)}, u32[]{:S(2)}) copy-start(bf16[1,3,6,96,1024]{4,3,2,1,0:T(8,128)(2,1)} %param.6) | copy-start | bytes 10616836
  9.9 29.3 %copy-start.3 = (s32[1024]{0:T(1024)S(1)}, s32[1024]{0:T(1024)}, u32[]{:S(2)}) copy-start(s32[1024]{0:T(1024)} %get-tuple-element.15) | copy-start | bytes 12292
  9.9 29.3 %copy-start.5 = (pred[1024]{0:T(1024)(128)(4,1)S(1)}, pred[1024]{0:T(1024)(128)(4,1)}, u32[]{:S(2)}) copy-start(pred[1024]{0:T(1024)(128)(4,1)} %get-tuple-element.16) | copy-start | bytes 3076
  9.9 29.4 %copy-start.6 = (pred[1024]{0:T(1024)(128)(4,1)S(1)}, pred[1024]{0:T(1024)(128)(4,1)}, u32[]{:S(2)}) copy-start(pred[1024]{0:T(1024)(128)(4,1)} %get-tuple-element.17) | copy-start | bytes 3076
  9.9 29.4 %copy-start.7 = (pred[1024]{0:T(1024)(128)(4,1)S(1)}, pred[1024]{0:T(1024)(128)(4,1)}, u32[]{:S(2)}) copy-start(pred[1024]{0:T(1024)(128)(4,1)} %get-tuple-element.18) | copy-start | bytes 3076
  9.9 29.4 %copy-start.8 = (pred[1024]{0:T(1024)(128)(4,1)S(1)}, pred[1024]{0:T(1024)(128)(4,1)}, u32[]{:S(2)}) copy-start(pred[1024]{0:T(1024)(128)(4,1)} %get-tuple-element.19) | copy-start | bytes 3076
  10.0 29.4 %copy-start.10 = (f32[1024]{0:T(1024)S(1)}, f32[1024]{0:T(1024)}, u32[]{:S(2)}) copy-start(f32[1024]{0:T(1024)} %param.7) | copy-start | bytes 12292
  85.0 120.8 %all-to-all-start = ((bf16[1,5,6,96,1024]{3,2,1,0,4:T(8,128)(2,1)}), bf16[1,5,6,96,1024]{3,2,1,0,4:T(8,128)(2,1)}, u32[]{:S(2)}, u32[]{:S(2)}) async-start(bf16[1,5,6,96,1024]{3,2,1,0,4:T(8,128)(2,1)} %pad_maximum_fusion), calls=%async_computation | async-start | bytes 20971520 | tf_op jit(solution)/shard_map/all_to_all | solution.py:72
  222.0 3.3 copy-start.1
  227.0 6.3 %copy-start.4 = (s32[384]{0:T(512)S(1)}, s32[384]{0:T(512)}, u32[]{:S(2)}) copy-start(s32[384]{0:T(512)} %get-tuple-element.23) | copy-start | bytes 4612
  227.0 6.3 %copy-start.11 = (f32[384]{0:T(512)S(1)}, f32[384]{0:T(512)}, u32[]{:S(2)}) copy-start(f32[384]{0:T(512)} %param.8) | copy-start | bytes 4612
  227.0 6.3 %copy-start.12 = (pred[384]{0:T(512)(128)(4,1)S(1)}, pred[384]{0:T(512)(128)(4,1)}, u32[]{:S(2)}) copy-start(pred[384]{0:T(512)(128)(4,1)} %get-tuple-element.24) | copy-start | bytes 1156
  227.0 6.3 %copy-start.13 = (pred[384]{0:T(512)(128)(4,1)S(1)}, pred[384]{0:T(512)(128)(4,1)}, u32[]{:S(2)}) copy-start(pred[384]{0:T(512)(128)(4,1)} %get-tuple-element.25) | copy-start | bytes 1156
  227.0 6.3 %copy-start.14 = (pred[384]{0:T(512)(128)(4,1)S(1)}, pred[384]{0:T(512)(128)(4,1)}, u32[]{:S(2)}) copy-start(pred[384]{0:T(512)(128)(4,1)} %get-tuple-element.26) | copy-start | bytes 1156
  227.0 6.3 %copy-start.15 = (pred[384]{0:T(512)(128)(4,1)S(1)}, pred[384]{0:T(512)(128)(4,1)}, u32[]{:S(2)}) copy-start(pred[384]{0:T(512)(128)(4,1)} %get-tuple-element.27) | copy-start | bytes 1156
  452.7 89.5 %all-to-all-start.2 = ((bf16[8,5,6,48,256]{4,0,2,1,3:T(8,128)(2,1)}), bf16[8,5,6,48,256]{4,0,2,1,3:T(8,128)(2,1)}, u32[]{:S(2)}, u32[]{:S(2)}) async-start(bf16[8,5,6,48,256]{4,0,2,1,3:T(8,128)(2,1)} %copy.46), calls=%async_computation.2 | async-start | bytes 11796480 | tf_op jit(solution)/shard_map/all_to_all | solution.py:80
  546.3 2.1 copy-start.9
where the time goes:
time: 571 us; the launch traced here: 560 us
  waiting for transfers between devices  194 us (34%)
  blocking collectives  183 us (32%)
  matrix products  78.6 us (14%)
  local copies, waits for them, and re-layouts  66.3 us (12%)
  other arithmetic  22.2 us (4%)
  starting transfers between devices  14.2 us (2%)
    all_to_all x1, blocking collectives, on_device(): lax.all_to_all(z_payload, 'snap', split_axis=3, concat_axis=0, tiled=True)  183 us
    all_to_all x1, waiting for transfers between devices, on_device(): lax.all_to_all(payload, 'py', split_axis=4, concat_axis=3, tiled=True)  112 us
    all_to_all x1, waiting for transfers between devices, on_device(): lax.all_to_all(lax.all_to_all(z_payload, 'snap', split_axis=3, concat_axi...  81.9 us
    dot_general x1, matrix products, apply_split(): jnp.einsum(form, fields, table_low, preferred_element_type=jnp.float32)  29.3 us
    dot_general x1, matrix products, apply_split(): jnp.einsum(form, fields, table_high, preferred_element_type=jnp.float32)  28.4 us
    all_to_all x2, local copies, waits for them, and re-layouts, on_device(): lax.all_to_all(payload, 'py', split_axis=4, concat_axis=3, tiled=True)  16.2 us
    all_to_all x1, local copies, waits for them, and re-layouts, on_device(): lax.all_to_all(z_payload, 'snap', split_axis=3, concat_axis=0, tiled=True)  12.2 us
    unnamed x35, local copies, waits for them, and re-layouts  11.7 us
  transfers between devices with their start and end apart: 2, of which 2 were waited for; matrix products, arithmetic and copies ran while one was open for 0% of the time, Pallas kernels for 0%

commit v1 on v0

--- a/solution.py
+++ b/solution.py
@@ -77,12 +77,20 @@
     slope_wy = y_slopes[:, 1].astype(jnp.bfloat16)
     spin_z = (ylines[:, 3].astype(jnp.float32) - slope_uy).astype(jnp.bfloat16)
     z_payload = jnp.stack([ylines[:, 0], ylines[:, 1], ylines[:, 4], slope_wy, spin_z], axis=1)
-    zlines = lax.all_to_all(
-        lax.all_to_all(z_payload, "snap", split_axis=3, concat_axis=0, tiled=True),
-        "pz",
-        split_axis=3,
-        concat_axis=2,
-        tiled=True,
+    zlines = jnp.concatenate(
+        lax.all_to_all(
+            jnp.stack(
+                jnp.split(
+                    lax.all_to_all(z_payload, "snap", split_axis=3, concat_axis=0, tiled=True),
+                    lax.axis_size("pz"),
+                    axis=3,
+                )
+            ),
+            "pz",
+            0,
+            0,
+        ),
+        axis=2,
     )
     vorticity = vorticity_from(zlines, metric_z)
     return jnp.einsum(

time: 571 us -> 570 us (level)
    all_to_all x1, local copies, waits for them, and re-layouts: 12.2 us -> 4.64 us  [on_device(): lax.all_to_all(z_payload, 'snap', split_axis=3, concat_axis=0, tiled=True)]
    unnamed x35 -> x42, local copies, waits for them, and re-layouts: 11.7 us -> 13.4 us
where the time goes in v1:
time: 570 us; the launch traced here: 559 us
  waiting for transfers between devices  194 us (34%)
  blocking collectives  183 us (32%)
  matrix products  78.7 us (14%)
  local copies, waits for them, and re-layouts  65.6 us (12%)
  other arithmetic  22.2 us (4%)
  starting transfers between devices  14.2 us (2%)
    all_to_all x1, blocking collectives, on_device(): lax.all_to_all(z_payload, 'snap', split_axis=3, concat_axis=0, tiled=True)  183 us
    all_to_all x1, waiting for transfers between devices, on_device(): lax.all_to_all(payload, 'py', split_axis=4, concat_axis=3, tiled=True)  112 us
    all_to_all x1, waiting for transfers between devices, on_device(): lax.all_to_all(jnp.stack(jnp.split(lax.all_to_all(z_payload, 'snap', spli...  81.9 us
    dot_general x1, matrix products, apply_split(): jnp.einsum(form, fields, table_low, preferred_element_type=jnp.float32)  29.3 us
    dot_general x1, matrix products, apply_split(): jnp.einsum(form, fields, table_high, preferred_element_type=jnp.float32)  28.4 us
    all_to_all x2, local copies, waits for them, and re-layouts, on_device(): lax.all_to_all(payload, 'py', split_axis=4, concat_axis=3, tiled=True)  16.2 us
    unnamed x42, local copies, waits for them, and re-layouts  13.4 us
  transfers between devices with their start and end apart: 2, of which 2 were waited for; matrix products, arithmetic and copies ran while one was open for 0% of the time, Pallas kernels for 0%

profile of v1, /device:TPU:30, one launch (start us, length us, event | category | flops | bytes accessed | tf_op | source)
XLA Modules:
  0.0 559.1 jit_solution(3593045733525880347)
XLA Ops:
  0.0 0.6 fusion.369
  0.6 0.6 fusion.375
  1.2 0.6 fusion.377
  1.8 8.1 %copy.34 = bf16[1,3,6,96,1024]{3,2,1,0,4:T(8,128)(2,1)} copy(bf16[1,3,6,96,1024]{4,3,2,1,0:T(8,128)(2,1)} %param.6) | data formatting | bytes 7077888 | tf_op args[0]
  10.0 29.3 %fusion.112 = f32[1024,2,6,96]{0,3,2,1:T(8,128)S(1)} fusion(s32[1024]{0:T(1024)S(1)} %get-tuple-element.12, s32[1024]{0:T(1024)S(1)} %get-tuple-element.13, s32[1024]{0:T(1024)S(1)} %get-tuple-element.14, s32[1024]{0:T(1024)} %get-tuple-element.15, pred[1024]{0:T(1024)(128)(4,1)} %get-tuple-element.19, pred[1024]{0:T(1024)(128)(4,1)} %get-tuple-element.18, ...), kind=kOutput, calls=%fused_computation.135 | convolution fusion | flops 2530213888 | bytes 7098368 | tf_op jit(solution)/shard_map/sczyj,ij->sczyi/dot_general | solution.py:50
  39.3 28.4 %fusion.104 = bf16[1,2,6,96,1024]{4,3,2,1,0:T(8,128)(2,1)} fusion(f32[1024,2,6,96]{0,3,2,1:T(8,128)S(1)} %fusion.112, f32[1024]{0:T(1024)S(1)} %copy-done.10, bf16[1,3,6,96,1024]{4,3,2,1,0:T(8,128)(2,1)S(1)} %copy-done.2, s32[1024]{0:T(1024)S(1)} %get-tuple-element.12, pred[1024]{0:T(1024)(128)(4,1)S(1)} %copy-done.8, s32[1024]{0:T(1024)S(1)} %get-tuple-element.13, ...), kind=kOutput, calls=%fused_computation.123 | convolution fusion | flops 2530607104 | bytes 9461760 | tf_op jit(solution)/shard_map/sczyj,ij->sczyi/dot_general | solution.py:49
  67.7 6.5 %copy.35 = bf16[1,2,6,96,1024]{3,2,1,0,4:T(8,128)(2,1)} copy(bf16[1,2,6,96,1024]{4,3,2,1,0:T(8,128)(2,1)} %fusion.104) | data formatting | bytes 4718592 | tf_op jit(solution)/shard_map/convert_element_type | solution.py:70
  74.2 10.8 %pad_maximum_fusion = bf16[1,5,6,96,1024]{3,2,1,0,4:T(8,128)(2,1)} fusion(bf16[1,2,6,96,1024]{3,2,1,0,4:T(8,128)(2,1)} %copy.35, bf16[1,3,6,96,1024]{3,2,1,0,4:T(8,128)(2,1)} %copy.34), kind=kLoop, calls=%fused_computation | loop fusion | flops 2949120 | bytes 11796480 | tf_op jit(solution)/shard_map/concatenate | solution.py:71
  85.0 6.8 %all-to-all-start = ((bf16[1,5,6,96,1024]{3,2,1,0,4:T(8,128)(2,1)}), bf16[1,5,6,96,1024]{3,2,1,0,4:T(8,128)(2,1)}, u32[]{:S(2)}, u32[]{:S(2)}) async-start(bf16[1,5,6,96,1024]{3,2,1,0,4:T(8,128)(2,1)} %pad_maximum_fusion), calls=%async_computation | async-start | bytes 20971520 | tf_op jit(solution)/shard_map/all_to_all | solution.py:72
  91.8 0.6 fusion.392
  92.4 0.6 fusion.394
  92.9 0.6 fusion.386
  93.5 112.3 %all-to-all-done = bf16[1,5,6,96,1024]{3,2,1,0,4:T(8,128)(2,1)} async-done(((bf16[1,5,6,96,1024]{3,2,1,0,4:T(8,128)(2,1)}), bf16[1,5,6,96,1024]{3,2,1,0,4:T(8,128)(2,1)}, u32[]{:S(2)}, u32[]{:S(2)}) %all-to-all-start) | async-done | bytes 5898272 | tf_op jit(solution)/shard_map/all_to_all | solution.py:72
  205.8 12.4 %copy.59 = bf16[1,5,6,96,4,256]{5,4,3,2,1,0:T(4,128)(2,1)} copy(bf16[1,5,6,96,4,256]{3,2,1,5,4,0:T(8,128)(2,1)} %bitcast.7) | data formatting | bytes 11796480 | tf_op jit(solution)/shard_map/all_to_all | solution.py:72
  218.2 3.9 copy.37
  222.0 1.7 fusion.455
  223.7 0.2 slice.55
  223.9 1.4 copy-done.1
  225.3 1.7 copy.61
  227.1 6.2 %fusion.108 = f32[2,6,256,384]{3,2,1,0:T(8,128)S(1)} fusion(bf16[1,5,6,384,256]{4,3,2,1,0:T(8,128)(2,1)} %bitcast.123, s32[384]{0:T(512)S(1)} %get-tuple-element.20, s32[384]{0:T(512)S(1)} %get-tuple-element.21, s32[384]{0:T(512)S(1)} %get-tuple-element.22, s32[384]{0:T(512)} %get-tuple-element.23, pred[384]{0:T(512)(128)(4,1)} %get-tuple-element.27, ...), kind=kOutput, calls=%fused_computation.131 | convolution fusion | flops 922042368 | bytes 7086592 | tf_op jit(solution)/shard_map/ij,sczjx->sczix/dot_general | solution.py:47
  233.4 6.4 %fusion = f32[1,2,6,384,256]{3,4,2,1,0:T(8,128)S(1)} fusion(f32[2,6,256,384]{3,2,1,0:T(8,128)S(1)} %fusion.108, f32[384]{0:T(512)S(1)} %copy-done.11, bf16[1,5,6,384,256]{4,3,2,1,0:T(8,128)(2,1)} %bitcast.124, s32[384]{0:T(512)S(1)} %get-tuple-element.20, pred[384]{0:T(512)(128)(4,1)S(1)} %copy-done.15, s32[384]{0:T(512)S(1)} %get-tuple-element.21, ...), kind=kOutput, calls=%fused_computation.15 | convolution fusion | flops 923959296 | bytes 11805696 | tf_op jit(solution)/shard_map/ij,sczjx->sczix/dot_general | solution.py:46
  239.8 1.2 slice.94
  240.9 1.4 fusion.107
  242.3 1.6 copy.41
  243.9 2.4 copy.40
  246.2 4.8 pad_maximum_fusion.1
  251.0 6.2 %copy.42 = bf16[1,5,6,384,256]{4,2,1,0,3:T(8,128)(2,1)S(1)} copy(bf16[1,5,6,384,256]{4,3,2,1,0:T(8,128)(2,1)} %pad_maximum_fusion.1) | data formatting | bytes 11796480 | tf_op jit(solution)/shard_map/stack | solution.py:79
  257.2 183.2 %all_to_all.41 = bf16[1,5,6,384,256]{4,2,1,0,3:T(8,128)(2,1)} all-to-all(bf16[1,5,6,384,256]{4,2,1,0,3:T(8,128)(2,1)S(1)} %copy.42), channel_id=1, replica_groups=mesh['snap'=8,'py'=4,'pz'=8] {'snap'}, dimensions={3} | all-to-all | bytes 11796480 | tf_op jit(solution)/shard_map/all_to_all | solution.py:84
  440.4 4.6 copy.43
  445.2 0.3 fusion.143
  445.5 0.3 fusion.142
  445.9 0.3 fusion.141
  446.2 0.3 fusion.139
  446.5 0.3 fusion.138
  446.9 0.2 fusion.137
  447.1 5.1 copy.44
  452.2 7.5 %all-to-all-start.2 = ((bf16[8,8,5,6,6,256]{5,1,4,3,2,0:T(8,128)(2,1)}), bf16[8,8,5,6,6,256]{5,1,4,3,2,0:T(8,128)(2,1)}, u32[]{:S(2)}, u32[]{:S(2)}) async-start(bf16[8,8,5,6,6,256]{5,1,4,3,2,0:T(8,128)(2,1)} %copy.44), calls=%async_computation.2 | async-start | bytes 11796480 | tf_op jit(solution)/shard_map/all_to_all | solution.py:81
  459.7 81.9 %all-to-all-done.2 = bf16[8,8,5,6,6,256]{5,1,4,3,2,0:T(8,128)(2,1)} async-done(((bf16[8,8,5,6,6,256]{5,1,4,3,2,0:T(8,128)(2,1)}), bf16[8,8,5,6,6,256]{5,1,4,3,2,0:T(8,128)(2,1)}, u32[]{:S(2)}, u32[]{:S(2)}) %all-to-all-start.2) | async-done | bytes 5898272 | tf_op jit(solution)/shard_map/all_to_all | solution.py:81
  541.7 3.2 copy.45
  544.9 0.2 slice.61
  545.0 0.2 fusion.454
  545.3 0.4 copy.65
  545.7 2.1 fusion.123
  547.8 2.2 multiply_bitcast_fusion
  550.0 1.3 fusion.106
  551.3 0.4 pad_maximum_fusion.2
  551.8 4.0 fusion.130
  555.8 2.9 copy.51
  (39 shorter events, 0.3 us)
Async XLA Ops:
  0.0 551.8 %copy-start = (f32[8,4]{0,1:T(4,128)S(1)}, f32[8,4]{0,1:T(4,128)}, u32[]{:S(2)}) copy-start(f32[8,4]{0,1:T(4,128)} %param.10) | copy-start | bytes 388
  1.8 8.1 %copy-start.2 = (bf16[1,3,6,96,1024]{4,3,2,1,0:T(8,128)(2,1)S(1)}, bf16[1,3,6,96,1024]{4,3,2,1,0:T(8,128)(2,1)}, u32[]{:S(2)}) copy-start(bf16[1,3,6,96,1024]{4,3,2,1,0:T(8,128)(2,1)} %param.6) | copy-start | bytes 10616836
  9.9 29.3 %copy-start.3 = (s32[1024]{0:T(1024)S(1)}, s32[1024]{0:T(1024)}, u32[]{:S(2)}) copy-start(s32[1024]{0:T(1024)} %get-tuple-element.15) | copy-start | bytes 12292
  9.9 29.3 %copy-start.5 = (pred[1024]{0:T(1024)(128)(4,1)S(1)}, pred[1024]{0:T(1024)(128)(4,1)}, u32[]{:S(2)}) copy-start(pred[1024]{0:T(1024)(128)(4,1)} %get-tuple-element.16) | copy-start | bytes 3076
  9.9 29.4 %copy-start.6 = (pred[1024]{0:T(1024)(128)(4,1)S(1)}, pred[1024]{0:T(1024)(128)(4,1)}, u32[]{:S(2)}) copy-start(pred[1024]{0:T(1024)(128)(4,1)} %get-tuple-element.17) | copy-start | bytes 3076
  9.9 29.4 %copy-start.7 = (pred[1024]{0:T(1024)(128)(4,1)S(1)}, pred[1024]{0:T(1024)(128)(4,1)}, u32[]{:S(2)}) copy-start(pred[1024]{0:T(1024)(128)(4,1)} %get-tuple-element.18) | copy-start | bytes 3076
  9.9 29.4 %copy-start.8 = (pred[1024]{0:T(1024)(128)(4,1)S(1)}, pred[1024]{0:T(1024)(128)(4,1)}, u32[]{:S(2)}) copy-start(pred[1024]{0:T(1024)(128)(4,1)} %get-tuple-element.19) | copy-start | bytes 3076
  10.0 29.4 %copy-start.10 = (f32[1024]{0:T(1024)S(1)}, f32[1024]{0:T(1024)}, u32[]{:S(2)}) copy-start(f32[1024]{0:T(1024)} %param.7) | copy-start | bytes 12292
  85.0 120.8 %all-to-all-start = ((bf16[1,5,6,96,1024]{3,2,1,0,4:T(8,128)(2,1)}), bf16[1,5,6,96,1024]{3,2,1,0,4:T(8,128)(2,1)}, u32[]{:S(2)}, u32[]{:S(2)}) async-start(bf16[1,5,6,96,1024]{3,2,1,0,4:T(8,128)(2,1)} %pad_maximum_fusion), calls=%async_computation | async-start | bytes 20971520 | tf_op jit(solution)/shard_map/all_to_all | solution.py:72
  222.0 3.3 copy-start.1
  227.0 6.3 %copy-start.4 = (s32[384]{0:T(512)S(1)}, s32[384]{0:T(512)}, u32[]{:S(2)}) copy-start(s32[384]{0:T(512)} %get-tuple-element.23) | copy-start | bytes 4612
  227.0 6.3 %copy-start.11 = (f32[384]{0:T(512)S(1)}, f32[384]{0:T(512)}, u32[]{:S(2)}) copy-start(f32[384]{0:T(512)} %param.8) | copy-start | bytes 4612
  227.0 6.3 %copy-start.12 = (pred[384]{0:T(512)(128)(4,1)S(1)}, pred[384]{0:T(512)(128)(4,1)}, u32[]{:S(2)}) copy-start(pred[384]{0:T(512)(128)(4,1)} %get-tuple-element.24) | copy-start | bytes 1156
  227.0 6.3 %copy-start.13 = (pred[384]{0:T(512)(128)(4,1)S(1)}, pred[384]{0:T(512)(128)(4,1)}, u32[]{:S(2)}) copy-start(pred[384]{0:T(512)(128)(4,1)} %get-tuple-element.25) | copy-start | bytes 1156
  227.0 6.3 %copy-start.14 = (pred[384]{0:T(512)(128)(4,1)S(1)}, pred[384]{0:T(512)(128)(4,1)}, u32[]{:S(2)}) copy-start(pred[384]{0:T(512)(128)(4,1)} %get-tuple-element.26) | copy-start | bytes 1156
  227.0 6.3 %copy-start.15 = (pred[384]{0:T(512)(128)(4,1)S(1)}, pred[384]{0:T(512)(128)(4,1)}, u32[]{:S(2)}) copy-start(pred[384]{0:T(512)(128)(4,1)} %get-tuple-element.27) | copy-start | bytes 1156
  452.2 89.5 %all-to-all-start.2 = ((bf16[8,8,5,6,6,256]{5,1,4,3,2,0:T(8,128)(2,1)}), bf16[8,8,5,6,6,256]{5,1,4,3,2,0:T(8,128)(2,1)}, u32[]{:S(2)}, u32[]{:S(2)}) async-start(bf16[8,8,5,6,6,256]{5,1,4,3,2,0:T(8,128)(2,1)} %copy.44), calls=%async_computation.2 | async-start | bytes 11796480 | tf_op jit(solution)/shard_map/all_to_all | solution.py:81
  545.7 2.2 copy-start.9
